TPU v7x, 256 devices: a whole 4x4x8 slice. The times are simulated.
256 devices in a mesh: seq: 8 (over z_hi, core), expert: 16 (over y, x), tensor: 2 (over z_lo).
Axes of the slice: x: 4, y: 4, z: 8 (z_hi: 4, z_lo: 2; z = z_hi * 2 + z_lo), core: 2. Of those that a mesh axis runs over, the one named last changes fastest.
Arguments:
- q_rows: bfloat16 [16, 1024, 4096], P('expert', 'seq', 'tensor'), may hold values from -6 to 6
- k_rows: bfloat16 [16, 1024, 512], P('expert', 'seq', 'tensor'), may hold values from -6 to 6
- value_rows: bfloat16 [16, 1024, 512], P('expert', 'seq', 'tensor'), may hold values from -6 to 6
- x_rows: bfloat16 [16, 1024, 2048], P('expert', 'seq'), may hold values from -40 to 40
- out_weight: bfloat16 [4096, 2048], P('tensor', 'expert'), may hold values from -0.09375 to 0.09375
- norm_gain: float32 [2048], P('tensor'), may hold values from 0.1 to 1.9
- w_gate: bfloat16 [128, 2048, 768], P(('seq', 'expert'), None, 'tensor'), may hold values from -0.125 to 0.125
- w_up: bfloat16 [128, 2048, 768], P(('seq', 'expert'), None, 'tensor'), may hold values from -0.125 to 0.125
- w_down: bfloat16 [128, 768, 2048], P(('seq', 'expert'), 'tensor'), may hold values from -0.21875 to 0.21875
- expert_ids: int32 [16, 1024, 8], P('expert', 'seq'), may hold values from 0 to 127, all different within a row; in each aligned block of 128 rows (0 to 127, 128 to 255, ..., all dimensions but the last counted through in order) at most 12 rows name the same one
- gate_weights: float32 [16, 1024, 8], P('expert', 'seq'), may hold values from 0.02 to 0.4
Outputs:
- layer_out: bfloat16 [16, 1024, 2048], P('expert', 'seq', 'tensor')
Inputs may be any that keep to these rules, and one draw needn't show every extreme that they name: `expert_ids`: in each token's row the 8 ids differ. Among the 128 tokens of one block of positions (the blocks laid session after session) no expert is named more than 12 times, a bound that some block reaches; every expert is named somewhere.
All inputs are finite; a program needn't handle non-finite values.
Results may differ from a plain program's by a relative error of at most 0.007.
Values may be sent and summed in bfloat16 or wider, within the bound.
A program may use at most 128 MiB of HBM per device.

v0:
```python
import math
import jax
import jax.numpy as jnp
from jax import lax
from jax.sharding import PartitionSpec as P

HEAD_SIZE = 128
TOPK = 8


def in_one_piece(arrays, axis, dim, along):
    widths = [a.shape[along] for a in arrays]
    both = jnp.concatenate(arrays, axis=along)
    out = lax.all_gather(both, axis, axis=dim, tiled=True)
    return tuple(jnp.split(out, [sum(widths[:k]) for k in range(1, len(widths))], axis=along))


def split_up(shard, dim, devices):
    before, after = (shard.shape[:dim], shard.shape[dim + 1 :])
    return jnp.moveaxis(shard.reshape(*before, devices, -1, *after), dim, 0)


def summed_on_arrival(shard, axis, dim):
    devices = lax.axis_size(axis)
    blocks = lax.all_to_all(split_up(shard, dim, devices), axis, 0, 0, tiled=True)
    return jnp.sum(blocks.astype(jnp.float32), axis=0)


def copy_for_each(shard, axis):
    copies = jnp.broadcast_to(shard, (lax.axis_size(axis), *shard.shape))
    return lax.all_to_all(copies, axis, split_axis=0, concat_axis=0, tiled=True)


def taken_together(shard, axis):
    everything = copy_for_each(shard, axis)
    return jnp.sum(everything, axis=0)


def joined_along(blocks, dim):
    blocks = jnp.moveaxis(blocks, 0, dim)
    dims = blocks.shape
    return blocks.reshape(*dims[:dim], dims[dim] * dims[dim + 1], *dims[dim + 2 :])


def one_exchange(shard, axis, axes, splits, concats):
    sizes = [lax.axis_size(a) for a in axes]
    blocks = split_up(shard, splits[0], sizes[0])
    blocks = jnp.moveaxis(split_up(blocks, splits[1] + 1, sizes[1]), 0, 1)
    inside = blocks.shape[2:]
    blocks = blocks.reshape(-1, *inside)
    blocks = lax.all_to_all(blocks, axis, split_axis=0, concat_axis=0, tiled=True)
    blocks = joined_along(blocks.reshape(*sizes, *inside), concats[0] + 1)
    return joined_along(blocks, concats[1])


def collect(shard, axis, dim):
    return joined_along(copy_for_each(shard, axis), dim)


def per_device(
    q_rows,
    k_rows,
    value_rows,
    x_rows,
    out_weight,
    norm_gain,
    w_gate,
    w_up,
    w_down,
    expert_ids,
    gate_weights,
):
    rows_here = q_rows.shape[1]
    kv_heads = k_rows.shape[2] // HEAD_SIZE
    q_heads = q_rows.shape[2] // HEAD_SIZE
    group_width = q_heads // kv_heads
    queries = q_rows[0].reshape(rows_here, kv_heads, group_width, HEAD_SIZE)
    offset = lax.axis_index("seq") * rows_here
    query_pos = offset + jnp.arange(rows_here, dtype=jnp.int32)
    softmax_scale = 1.0 / math.sqrt(HEAD_SIZE)
    tensor_pos = lax.axis_index("tensor")
    tensor_count = lax.axis_size("tensor")
    full_gate, full_up = in_one_piece((w_gate[0], w_up[0]), "tensor", 1, 0)
    full_down = lax.all_gather(w_down[0], "tensor", axis=0, tiled=True)
    pieces = in_one_piece((k_rows, value_rows), "seq", 1, 0)
    running_max = jnp.full((kv_heads, group_width, rows_here), -1e30, jnp.float32)
    block_rows = pieces[0].shape[1]
    key_block = pieces[0][0].reshape(block_rows, kv_heads, HEAD_SIZE)
    value_block = pieces[1][0].reshape(block_rows, kv_heads, HEAD_SIZE)
    scores = (
        jnp.einsum("igrd,jgd->grij", queries, key_block, preferred_element_type=jnp.float32)
        * softmax_scale
    )
    key_pos = jnp.arange(block_rows, dtype=jnp.int32)
    allowed = key_pos[None, :] <= query_pos[:, None]
    scores = jnp.where(allowed, scores, jnp.float32(-1e30))
    new_max = jnp.maximum(running_max, jnp.max(scores, axis=-1))
    weights = jnp.where(allowed, jnp.exp(scores - new_max[..., None]), jnp.float32(0.0))
    running_sum = jnp.sum(weights, axis=-1)
    weighted = jnp.einsum(
        "grij,jgd->grid",
        weights.astype(jnp.bfloat16),
        value_block,
        preferred_element_type=jnp.float32,
    )
    running_max, running_sum, weighted = (new_max, running_sum, weighted)
    attn_rows = (
        (weighted / running_sum[..., None])
        .transpose(2, 0, 1, 3)
        .reshape(rows_here, q_heads * HEAD_SIZE)
        .astype(jnp.bfloat16)
    )
    head_terms = jnp.dot(
        attn_rows,
        lax.all_gather(out_weight, "expert", axis=1, tiled=True),
        preferred_element_type=jnp.float32,
    )
    width = x_rows.shape[2]
    half_width = width // tensor_count
    share_sum = summed_on_arrival(head_terms.astype(jnp.bfloat16), "tensor", 1)
    mixed_half = (
        lax.dynamic_slice_in_dim(x_rows[0], tensor_pos * half_width, half_width, 1).astype(
            jnp.float32
        )
        + share_sum
    )
    power = taken_together(jnp.sum(mixed_half * mixed_half, axis=1), "tensor")
    inverse = lax.rsqrt(power / width + 1e-06)
    normed = (mixed_half * inverse[:, None] * norm_gain[None, :]).astype(jnp.bfloat16)
    seq_count = lax.axis_size("seq")
    group_count = lax.axis_size("expert")
    experts = seq_count * group_count
    capacity = max(2, 3 * rows_here * TOPK // (2 * experts))
    routed = expert_ids[0].reshape(-1)
    assigned = routed.shape[0]
    member = (routed[:, None] == jnp.arange(experts, dtype=jnp.int32)[None, :]).astype(jnp.int32)
    earlier = jnp.cumsum(member, axis=0) - member
    slot_index = jnp.sum(earlier * member, axis=1)
    target = routed * capacity + slot_index
    owner_index = (
        jnp.full((experts * capacity,), assigned, jnp.int32)
        .at[target]
        .set(jnp.arange(assigned, dtype=jnp.int32))
    )
    filled = owner_index < assigned
    source = jnp.minimum(owner_index // TOPK, rows_here - 1)
    whole_normed = collect(normed, "tensor", 1)
    outgoing = jnp.where(
        filled[:, None], whole_normed[source], jnp.zeros((), jnp.bfloat16)
    ).reshape(experts, capacity, width)
    half_cap = capacity // tensor_count
    my_slots = lax.dynamic_slice_in_dim(outgoing, tensor_pos * half_cap, half_cap, 1)
    hidden_half = full_down.shape[0] // tensor_count
    grouped = my_slots.reshape((seq_count, group_count) + my_slots.shape[1:])
    arrived = one_exchange(grouped, ("seq", "expert"), ("seq", "expert"), (0, 1), (0, 1))
    whole_arrived = arrived.reshape((experts,) + my_slots.shape[1:])
    flat_rows = whole_arrived.reshape(-1, width)
    gate_act = jnp.dot(flat_rows, full_gate, preferred_element_type=jnp.float32)
    up_act = jnp.dot(flat_rows, full_up, preferred_element_type=jnp.float32)
    hidden = (jax.nn.silu(gate_act) * up_act).astype(jnp.bfloat16)
    total = jnp.zeros((flat_rows.shape[0], width), jnp.float32)
    for group_pos in range(tensor_count):
        lo_col = group_pos * hidden_half
        piece = jnp.dot(
            hidden[:, lo_col : lo_col + hidden_half],
            full_down[lo_col : lo_col + hidden_half],
            preferred_element_type=jnp.float32,
        )
        total = total + piece.astype(jnp.bfloat16).astype(jnp.float32)
    finished = total.astype(jnp.bfloat16).reshape(whole_arrived.shape)
    finished = finished.reshape((seq_count, group_count) + finished.shape[1:])
    returned = one_exchange(finished, ("seq", "expert"), ("seq", "expert"), (0, 1), (0, 1))
    back_whole = returned.reshape((experts,) + returned.shape[2:])
    returned = lax.all_to_all(back_whole, "tensor", split_axis=2, concat_axis=1, tiled=True)
    came_back = returned.reshape(experts * capacity, half_width)
    picked = came_back[target].astype(jnp.float32)
    weights_flat = gate_weights[0].reshape(-1)
    blended = jnp.sum((picked * weights_flat[:, None]).reshape(rows_here, TOPK, half_width), axis=1)
    return (mixed_half + blended).astype(jnp.bfloat16)[None]


def solution(mesh):
    return jax.shard_map(
        per_device,
        mesh=mesh,
        in_specs=(
            P("expert", "seq", "tensor"),
            P("expert", "seq", "tensor"),
            P("expert", "seq", "tensor"),
            P("expert", "seq", None),
            P("tensor", "expert"),
            P("tensor"),
            P(("seq", "expert"), None, "tensor"),
            P(("seq", "expert"), None, "tensor"),
            P(("seq", "expert"), "tensor", None),
            P("expert", "seq", None),
            P("expert", "seq", None),
        ),
        out_specs=P("expert", "seq", "tensor"),
        check_vma=False,
    )
```

profile of v0, /device:TPU:1, one launch (start us, length us, event | category | flops | bytes accessed | tf_op | source)
XLA Modules:
  0.0 554.6 jit_solution(8807647525143231353)
XLA Ops:
  6.5 0.9 copy.93
  7.5 1.0 copy.94
  8.5 0.7 pad_maximum_fusion.1
  9.1 0.0 all-gather.6.cloned.1.call-update
  9.2 0.0 all-gather.8.cloned.1.call-start
  9.2 0.7 all-gather.8.cloned.1.call-update
  9.9 0.0 all-gather.10.cloned.1.call-start
  10.0 3.9 pad_maximum_fusion
  13.9 0.1 copy.100
  14.0 0.1 eq.29
  14.1 0.1 eq.25
  14.2 0.1 iota_compare_fusion.2
  14.3 0.1 copy.119
  14.5 0.1 copy.102
  14.6 0.2 fusion.28
  14.8 30.4 %all-gather.6.cloned.1.call-done = bf16[2,1024,256]{1,2,0:T(8,128)(2,1)} async-done(((bf16[2,128,256]{1,2,0:T(8,128)(2,1)}), bf16[2,1024,256]{1,2,0:T(8,128)(2,1)}) %all-gather.6.cloned.1.call-update) | async-done | bytes 1048592 | tf_op jit(solution)/shard_map/all_gather | solution.py:14
  45.2 1.3 fusion.39
  46.5 1.5 fusion
  48.0 2.0 fusion.1
  50.0 2.1 divide_convert_fusion
  52.1 76.2 %all-gather.8.cloned.1.call-done = bf16[2048,2048]{1,0:T(8,128)(2,1)} async-done(((bf16[2048,128]{1,0:T(8,128)(2,1)}), bf16[2048,2048]{1,0:T(8,128)(2,1)}) %all-gather.8.cloned.1.call-update) | async-done | bytes 8388624 | tf_op jit(solution)/shard_map/all_gather | solution.py:115
  128.3 4.7 convolution_convert_fusion.2
  133.0 0.8 copy.125
  133.8 3.5 all-to-all-start
  137.4 0.1 copy.103
  137.5 0.1 copy.99
  137.6 0.1 mul.81
  137.7 0.4 fusion.25
  138.1 5.7 %all-to-all-done = bf16[2,128,1024]{2,1,0:T(8,128)(2,1)S(1)} async-done(((bf16[2,128,1024]{2,1,0:T(8,128)(2,1)}), bf16[2,128,1024]{2,1,0:T(8,128)(2,1)S(1)}, u32[]{:S(2)}, u32[]{:S(2)}) %all-to-all-start) | async-done | bytes 524320 | tf_op jit(solution)/shard_map/all_to_all | solution.py:25
  143.8 0.1 convert_reduce_fusion
  143.9 0.2 multiply_reduce_fusion
  144.0 0.6 broadcast_in_dim.55
  144.6 3.2 all-to-all-start.1
  147.9 4.3 scatter_custom_fusion
  152.2 0.1 multiply_convert_fusion.1
  152.4 0.9 broadcast_in_dim.56
  153.2 3.7 all-to-all-start.2
  156.9 0.1 broadcast_in_dim.53
  157.1 0.1 constant_dynamic-slice_fusion
  157.2 12.9 %all-to-all-done.2 = bf16[2,128,1024]{2,1,0:T(8,128)(2,1)S(1)} async-done(((bf16[2,128,1024]{2,1,0:T(8,128)(2,1)}), bf16[2,128,1024]{2,1,0:T(8,128)(2,1)S(1)}, u32[]{:S(2)}, u32[]{:S(2)}) %all-to-all-start.2) | async-done | bytes 524320 | tf_op jit(solution)/shard_map/all_to_all | solution.py:31
  170.2 7.1 %gather_fusion = bf16[1536,2048]{1,0:T(8,128)(2,1)} fusion(bf16[128,2048]{1,0:T(8,128)(2,1)S(1)} %bitcast.108, s32[2048]{0:T(1024)S(1)} %pad_clamp_fusion), kind=kCustom, calls=%fused_computation | custom fusion | bytes 12589056 | tf_op jit(solution)/shard_map/gather | solution.py:149
  177.2 10.6 %gather.9 = bf16[128,12,2048]{2,1,0:T(8,128)(2,1)} reshape(bf16[1536,2048]{1,0:T(8,128)(2,1)} %gather_fusion) | data formatting | bytes 12582912 | tf_op jit(solution)/shard_map/gather | solution.py:149
  187.8 6.0 %fusion.3 = bf16[128,1,1,6,2048]{4,3,2,1,0:T(8,128)(2,1)} fusion(bf16[128,12,2048]{2,1,0:T(8,128)(2,1)} %gather.9, s32[]{:T(128)S(6)} %select_n.44, pred[128,6]{1,0:T(8,128)(4,1)S(1)} %constant_dynamic-slice_fusion), kind=kLoop, calls=%fused_computation.10 | loop fusion | flops 1572864 | bytes 6292228 | tf_op jit(solution)/shard_map/reshape;transpose;transpose;reshape;reshape;reshape | solution.py:50
  193.8 15.1 %all-to-all-start.3 = ((bf16[128,1,1,6,2048]{4,3,2,1,0:T(8,128)(2,1)}), bf16[128,1,1,6,2048]{4,3,2,1,0:T(8,128)(2,1)}, u32[]{:S(2)}, u32[]{:S(2)}) async-start(bf16[128,1,1,6,2048]{4,3,2,1,0:T(8,128)(2,1)} %fusion.3), calls=%async_computation.3 | async-start | bytes 8388608 | tf_op jit(solution)/shard_map/all_to_all | solution.py:51
  208.9 0.0 all-gather.12.cloned.1.call-start
  208.9 0.5 all-gather.12.cloned.1.call-update
  209.4 127.5 %all-to-all-done.3 = bf16[128,1,1,6,2048]{4,3,2,1,0:T(8,128)(2,1)} async-done(((bf16[128,1,1,6,2048]{4,3,2,1,0:T(8,128)(2,1)}), bf16[128,1,1,6,2048]{4,3,2,1,0:T(8,128)(2,1)}, u32[]{:S(2)}, u32[]{:S(2)}) %all-to-all-start.3) | async-done | bytes 3145760 | tf_op jit(solution)/shard_map/all_to_all | solution.py:51
  336.9 4.9 reshape_reshape_reshape.3
  341.8 0.0 all-gather.10.cloned.1.call-done
  341.8 4.6 fusion.10
  346.5 3.8 multiply_convert_fusion
  350.3 3.5 convolution_convert_fusion
  353.8 1.8 add_convert_fusion
  355.6 2.9 reshape_transpose_transpose_reshape_reshape_reshape_reshape.3
  358.5 107.2 %all_to_all.41 = bf16[128,1,1,6,2048]{4,3,2,1,0:T(8,128)(2,1)} all-to-all(bf16[128,1,1,6,2048]{4,3,2,1,0:T(8,128)(2,1)} %bitcast.109), channel_id=1, replica_groups=mesh['seq'=8,'expert'=16,'tensor'=2] {'seq','expert'}, dimensions={0} | all-to-all | bytes 6291456 | tf_op jit(solution)/shard_map/all_to_all | solution.py:51
  465.7 7.2 %copy.108 = bf16[128,6,2048]{0,1,2:T(8,128)(2,1)} copy(bf16[128,6,2048]{2,1,0:T(8,128)(2,1)} %bitcast.111) | data formatting | bytes 6291456 | tf_op jit(solution)/shard_map/reshape;reshape | solution.py:173
  472.9 6.0 %all-to-all-start.5 = ((bf16[128,6,2048]{0,1,2:T(8,128)(2,1)}), bf16[128,6,2048]{0,1,2:T(8,128)(2,1)}, u32[]{:S(2)}, u32[]{:S(2)}) async-start(bf16[128,6,2048]{0,1,2:T(8,128)(2,1)} %copy.108), calls=%async_computation.5 | async-start | bytes 8388608 | tf_op jit(solution)/shard_map/all_to_all | solution.py:174
  478.9 0.1 copy.110
  479.0 46.5 %all-to-all-done.5 = bf16[128,6,2048]{0,1,2:T(8,128)(2,1)} async-done(((bf16[128,6,2048]{0,1,2:T(8,128)(2,1)}), bf16[128,6,2048]{0,1,2:T(8,128)(2,1)}, u32[]{:S(2)}, u32[]{:S(2)}) %all-to-all-start.5) | async-done | bytes 3145760 | tf_op jit(solution)/shard_map/all_to_all | solution.py:174
  525.5 7.4 %copy.109 = bf16[128,6,2,1024]{3,1,2,0:T(8,128)(2,1)} copy(bf16[128,6,2,1024]{0,1,3,2:T(8,128)(2,1)} %bitcast.35) | data formatting | bytes 6291456 | tf_op jit(solution)/shard_map/all_to_all | solution.py:174
  533.0 4.9 reshape.117
  537.8 5.3 gather_fusion.1
  543.2 2.9 fusion.4
  546.1 1.9 fusion.22
  (41 shorter events, 0.3 us)
Async XLA Ops:
  6.5 38.7 %all-gather.6.cloned.1.call-start = ((), (), s32[]{:S(2)}) async-start(), calls=%async_computation.6 | async-start | bytes 1179648 | tf_op jit(solution)/shard_map/all_gather | solution.py:14
  9.2 119.1 %all-gather.8.cloned.1.call-start = ((), (), s32[]{:S(2)}) async-start(), calls=%async_computation.7 | async-start | bytes 8912896 | tf_op jit(solution)/shard_map/all_gather | solution.py:115
  9.9 331.9 %all-gather.10.cloned.1.call-start = ((), (), s32[]{:S(2)}) async-start(), calls=%async_computation.8 | async-start | bytes 9437184 | tf_op jit(solution)/shard_map/all_gather | solution.py:14
  10.0 4.0 copy-start.4
  10.0 4.4 copy-start.2
  14.8 33.1 %copy-start.3 = (s32[128,9]{0,1:T(8,128)}, s32[128,9]{0,1:T(8,128)S(1)}, u32[]{:S(2)}) copy-start(s32[128,9]{0,1:T(8,128)S(1)} %reduce-window.9) | copy-start | bytes 13828
  128.3 9.0 %slice-start = ((s32[128,9]{0,1:T(8,128)}), s32[128,8]{0,1:T(8,128)S(1)}, s32[]{:S(2)}) async-start(s32[128,9]{0,1:T(8,128)} %copy-done.3), calls=%async_computation.10 | async-start | bytes 8192 | tf_op jit(solution)/shard_map/slice.1
  133.0 10.9 %copy-start.1 = (bf16[1,128,2048]{2,1,0:T(8,128)(2,1)S(1)}, bf16[1,128,2048]{2,1,0:T(8,128)(2,1)}, u32[]{:S(2)}) copy-start(bf16[1,128,2048]{2,1,0:T(8,128)(2,1)} %param.14) | copy-start | bytes 1572868
  133.0 19.2 %copy-start.5 = (f32[1024]{0:T(1024)S(1)}, f32[1024]{0:T(1024)}, u32[]{:S(2)}) copy-start(f32[1024]{0:T(1024)} %param.16) | copy-start | bytes 12292
  133.8 9.9 %all-to-all-start = ((bf16[2,128,1024]{2,1,0:T(8,128)(2,1)}), bf16[2,128,1024]{2,1,0:T(8,128)(2,1)S(1)}, u32[]{:S(2)}, u32[]{:S(2)}) async-start(bf16[2,128,1024]{2,1,0:T(8,128)(2,1)} %bitcast.107), calls=%async_computation | async-start | bytes 1048576 | tf_op jit(solution)/shard_map/all_to_all | solution.py:25
  143.9 26.2 %copy-start = (f32[128,1024]{1,0:T(8,128)}, f32[128,1024]{1,0:T(8,128)S(1)}, u32[]{:S(2)}) copy-start(f32[128,1024]{1,0:T(8,128)S(1)} %convert_reduce_fusion) | copy-start | bytes 1572868
  144.6 7.6 %all-to-all-start.1 = ((f32[2,1,128]{2,1,0:T(1,128)}), f32[2,1,128]{2,1,0:T(1,128)S(1)}, u32[]{:S(2)}, u32[]{:S(2)}) async-start(f32[2,1,128]{2,1,0:T(1,128)} %broadcast_in_dim.55), calls=%async_computation.1 | async-start | bytes 2048 | tf_op jit(solution)/shard_map/all_to_all | solution.py:31
  153.2 16.9 %all-to-all-start.2 = ((bf16[2,128,1024]{2,1,0:T(8,128)(2,1)}), bf16[2,128,1024]{2,1,0:T(8,128)(2,1)S(1)}, u32[]{:S(2)}, u32[]{:S(2)}) async-start(bf16[2,128,1024]{2,1,0:T(8,128)(2,1)} %broadcast_in_dim.56), calls=%async_computation.2 | async-start | bytes 1048576 | tf_op jit(solution)/shard_map/all_to_all | solution.py:31
  193.8 143.1 %all-to-all-start.3 = ((bf16[128,1,1,6,2048]{4,3,2,1,0:T(8,128)(2,1)}), bf16[128,1,1,6,2048]{4,3,2,1,0:T(8,128)(2,1)}, u32[]{:S(2)}, u32[]{:S(2)}) async-start(bf16[128,1,1,6,2048]{4,3,2,1,0:T(8,128)(2,1)} %fusion.3), calls=%async_computation.3 | async-start | bytes 8388608 | tf_op jit(solution)/shard_map/all_to_all | solution.py:51
  208.9 141.4 %all-gather.12.cloned.1.call-start = ((), (), s32[]{:S(2)}) async-start(), calls=%async_computation.9 | async-start | bytes 4718592 | tf_op jit(solution)/shard_map/all_gather | solution.py:84
  341.8 4.7 copy-start.7
  350.3 3.5 copy-start.8
  350.3 3.5 copy-start.9
  472.9 6.0 %copy-start.6 = (f32[1,128,8]{1,2,0:T(8,128)S(1)}, f32[1,128,8]{1,2,0:T(8,128)}, u32[]{:S(2)}) copy-start(f32[1,128,8]{1,2,0:T(8,128)} %param.21) | copy-start | bytes 12292
  472.9 52.6 %all-to-all-start.5 = ((bf16[128,6,2048]{0,1,2:T(8,128)(2,1)}), bf16[128,6,2048]{0,1,2:T(8,128)(2,1)}, u32[]{:S(2)}, u32[]{:S(2)}) async-start(bf16[128,6,2048]{0,1,2:T(8,128)(2,1)} %copy.108), calls=%async_computation.5 | async-start | bytes 8388608 | tf_op jit(solution)/shard_map/all_to_all | solution.py:174
Sparse Core Ops, SparseCore 0:
  9.3 35.8 all-gather.5
  47.6 80.6 all-gather.7
  130.1 131.7 all-gather.9
  263.6 81.7 all-gather.11
where the time goes:
time: 556 us; the launch traced here: 555 us
  waiting for transfers between devices  300 us (54%)
  blocking collectives  107 us (19%)
  local copies, waits for them, and re-layouts  61.2 us (11%)
  starting transfers between devices  31.5 us (6%)
  matrix products  22 us (4%)
  other arithmetic  18.6 us (3%)
  between operations  13.6 us (2%)
    all_to_all x1, waiting for transfers between devices, one_exchange(): lax.all_to_all(blocks, axis, split_axis=0, concat_axis=0, tiled=True)  127 us
    all_to_all x1, blocking collectives, one_exchange(): lax.all_to_all(blocks, axis, split_axis=0, concat_axis=0, tiled=True)  107 us
    all_gather x1, waiting for transfers between devices, per_device(): lax.all_gather(out_weight, 'expert', axis=1, tiled=True)  76.2 us
    all_to_all x1, waiting for transfers between devices, per_device(): lax.all_to_all(back_whole, 'tensor', split_axis=2, concat_axis=1, tiled=T...  46.5 us
    all_gather x2, waiting for transfers between devices, in_one_piece(): out = lax.all_gather(both, axis, axis=dim, tiled=True)  30.4 us
    gather x2, local copies, waits for them, and re-layouts, per_device(): whole_normed[source]  17.7 us
    all_to_all x1, starting transfers between devices, one_exchange(): lax.all_to_all(blocks, axis, split_axis=0, concat_axis=0, tiled=True)  15.1 us
    all_to_all x2, waiting for transfers between devices, copy_for_each(): return lax.all_to_all(copies, axis, split_axis=0, concat_axis=0, tiled=True)  13 us
  transfers between devices with their start and end apart: 9, of which 6 were waited for; matrix products, arithmetic and copies ran while one was open for 11% of the time, Pallas kernels for 0%

commit v1 on v0

--- a/solution.py
+++ b/solution.py
@@ -171,7 +171,12 @@
     finished = finished.reshape((seq_count, group_count) + finished.shape[1:])
     returned = one_exchange(finished, ("seq", "expert"), ("seq", "expert"), (0, 1), (0, 1))
     back_whole = returned.reshape((experts,) + returned.shape[2:])
-    returned = lax.all_to_all(back_whole, "tensor", split_axis=2, concat_axis=1, tiled=True)
+    returned = jnp.concatenate(
+        lax.all_to_all(
+            jnp.stack(jnp.split(back_whole, lax.axis_size("tensor"), axis=2)), "tensor", 0, 0
+        ),
+        axis=1,
+    )
     came_back = returned.reshape(experts * capacity, half_width)
     picked = came_back[target].astype(jnp.float32)
     weights_flat = gate_weights[0].reshape(-1)

time: 556 us -> 536 us (0.964)
  waiting for transfers between devices: 300 us -> 289 us
  local copies, waits for them, and re-layouts: 61.2 us -> 53.1 us
    all_to_all x1, waiting for transfers between devices: 46.5 us -> 35.3 us  [per_device(): lax.all_to_all(jnp.stack(jnp.split(back_whole, lax.axis_size('tensor'), a...]
    all_to_all x1 -> x0, local copies, waits for them, and re-layouts: 7.42 us -> none  [per_device(): lax.all_to_all(back_whole, 'tensor', split_axis=2, concat_axis=1, tiled=T...]
where the time goes in v1:
time: 536 us; the launch traced here: 535 us
  waiting for transfers between devices  289 us (54%)
  blocking collectives  107 us (20%)
  local copies, waits for them, and re-layouts  53.1 us (10%)
  starting transfers between devices  29.8 us (6%)
  matrix products  22 us (4%)
  other arithmetic  20.4 us (4%)
  between operations  13.6 us (3%)
    all_to_all x1, waiting for transfers between devices, one_exchange(): lax.all_to_all(blocks, axis, split_axis=0, concat_axis=0, tiled=True)  127 us
    all_to_all x1, blocking collectives, one_exchange(): lax.all_to_all(blocks, axis, split_axis=0, concat_axis=0, tiled=True)  107 us
    all_gather x1, waiting for transfers between devices, per_device(): lax.all_gather(out_weight, 'expert', axis=1, tiled=True)  76.2 us
    all_to_all x1, waiting for transfers between devices, per_device(): lax.all_to_all(jnp.stack(jnp.split(back_whole, lax.axis_size('tensor'), a...  35.3 us
    all_gather x2, waiting for transfers between devices, in_one_piece(): out = lax.all_gather(both, axis, axis=dim, tiled=True)  29.8 us
    gather x2, local copies, waits for them, and re-layouts, per_device(): whole_normed[source]  17.7 us
    all_to_all x1, starting transfers between devices, one_exchange(): lax.all_to_all(blocks, axis, split_axis=0, concat_axis=0, tiled=True)  15.1 us
    all_to_all x2, waiting for transfers between devices, copy_for_each(): return lax.all_to_all(copies, axis, split_axis=0, concat_axis=0, tiled=True)  13 us
  transfers between devices with their start and end apart: 9, of which 6 were waited for; matrix products, arithmetic and copies ran while one was open for 11% of the time, Pallas kernels for 0%

profile of v1, /device:TPU:1, one launch (start us, length us, event | category | flops | bytes accessed | tf_op | source)
XLA Modules:
  0.0 534.7 jit_solution(11986623177749765639)
XLA Ops:
  6.5 0.9 copy.61
  7.5 1.0 copy.62
  8.5 0.7 pad_maximum_fusion.2
  9.2 0.0 all-gather.8.cloned.1.call-start
  9.2 0.7 all-gather.8.cloned.1.call-update
  10.0 3.9 pad_maximum_fusion
  13.8 0.7 copy-done.4
  14.5 0.1 copy.68
  14.6 0.1 eq.29
  14.7 0.1 eq.25
  14.8 0.1 iota_compare_fusion.2
  14.9 0.1 copy.85
  15.0 0.1 copy.70
  15.1 0.2 fusion.28
  15.4 29.8 %all-gather.6.cloned.1.call-done = bf16[2,1024,256]{1,2,0:T(8,128)(2,1)} async-done(((bf16[2,128,256]{1,2,0:T(8,128)(2,1)}), bf16[2,1024,256]{1,2,0:T(8,128)(2,1)}) %all-gather.6.cloned.1.call-update) | async-done | bytes 1048592 | tf_op jit(solution)/shard_map/all_gather | solution.py:14
  45.2 1.3 fusion.39
  46.5 1.5 fusion
  48.0 2.0 fusion.1
  50.0 2.1 divide_convert_fusion
  52.1 76.2 %all-gather.8.cloned.1.call-done = bf16[2048,2048]{1,0:T(8,128)(2,1)} async-done(((bf16[2048,128]{1,0:T(8,128)(2,1)}), bf16[2048,2048]{1,0:T(8,128)(2,1)}) %all-gather.8.cloned.1.call-update) | async-done | bytes 8388624 | tf_op jit(solution)/shard_map/all_gather | solution.py:115
  128.3 4.7 convolution_convert_fusion.2
  133.0 0.8 copy.91
  133.8 3.5 all-to-all-start
  137.4 0.1 copy.71
  137.5 0.1 copy.67
  137.6 0.1 mul.81
  137.7 0.4 fusion.25
  138.1 5.7 %all-to-all-done = bf16[2,128,1024]{2,1,0:T(8,128)(2,1)S(1)} async-done(((bf16[2,128,1024]{2,1,0:T(8,128)(2,1)}), bf16[2,128,1024]{2,1,0:T(8,128)(2,1)S(1)}, u32[]{:S(2)}, u32[]{:S(2)}) %all-to-all-start) | async-done | bytes 524320 | tf_op jit(solution)/shard_map/all_to_all | solution.py:25
  143.8 0.1 convert_reduce_fusion
  143.9 0.2 multiply_reduce_fusion
  144.0 0.6 broadcast_in_dim.55
  144.6 3.2 all-to-all-start.1
  147.9 4.3 scatter_custom_fusion
  152.2 0.1 multiply_convert_fusion.1
  152.4 0.9 broadcast_in_dim.56
  153.2 3.7 all-to-all-start.2
  156.9 0.1 broadcast_in_dim.53
  157.1 0.1 constant_dynamic-slice_fusion
  157.2 12.9 %all-to-all-done.2 = bf16[2,128,1024]{2,1,0:T(8,128)(2,1)S(1)} async-done(((bf16[2,128,1024]{2,1,0:T(8,128)(2,1)}), bf16[2,128,1024]{2,1,0:T(8,128)(2,1)S(1)}, u32[]{:S(2)}, u32[]{:S(2)}) %all-to-all-start.2) | async-done | bytes 524320 | tf_op jit(solution)/shard_map/all_to_all | solution.py:31
  170.2 7.1 %gather_fusion = bf16[1536,2048]{1,0:T(8,128)(2,1)} fusion(bf16[128,2048]{1,0:T(8,128)(2,1)S(1)} %bitcast.113, s32[2048]{0:T(1024)S(1)} %pad_clamp_fusion), kind=kCustom, calls=%fused_computation | custom fusion | bytes 12589056 | tf_op jit(solution)/shard_map/gather | solution.py:149
  177.2 10.6 %gather.9 = bf16[128,12,2048]{2,1,0:T(8,128)(2,1)} reshape(bf16[1536,2048]{1,0:T(8,128)(2,1)} %gather_fusion) | data formatting | bytes 12582912 | tf_op jit(solution)/shard_map/gather | solution.py:149
  187.9 6.0 %fusion.3 = bf16[128,1,1,6,2048]{4,3,2,1,0:T(8,128)(2,1)} fusion(bf16[128,12,2048]{2,1,0:T(8,128)(2,1)} %gather.9, s32[]{:T(128)S(6)} %select_n.44, pred[128,6]{1,0:T(8,128)(4,1)S(1)} %constant_dynamic-slice_fusion), kind=kLoop, calls=%fused_computation.10 | loop fusion | flops 1572864 | bytes 6292228 | tf_op jit(solution)/shard_map/reshape;transpose;transpose;reshape;reshape;reshape | solution.py:50
  193.8 15.1 %all-to-all-start.3 = ((bf16[128,1,1,6,2048]{4,3,2,1,0:T(8,128)(2,1)}), bf16[128,1,1,6,2048]{4,3,2,1,0:T(8,128)(2,1)}, u32[]{:S(2)}, u32[]{:S(2)}) async-start(bf16[128,1,1,6,2048]{4,3,2,1,0:T(8,128)(2,1)} %fusion.3), calls=%async_computation.3 | async-start | bytes 8388608 | tf_op jit(solution)/shard_map/all_to_all | solution.py:51
  208.9 0.0 all-gather.12.cloned.1.call-start
  208.9 0.5 all-gather.12.cloned.1.call-update
  209.5 127.5 %all-to-all-done.3 = bf16[128,1,1,6,2048]{4,3,2,1,0:T(8,128)(2,1)} async-done(((bf16[128,1,1,6,2048]{4,3,2,1,0:T(8,128)(2,1)}), bf16[128,1,1,6,2048]{4,3,2,1,0:T(8,128)(2,1)}, u32[]{:S(2)}, u32[]{:S(2)}) %all-to-all-start.3) | async-done | bytes 3145760 | tf_op jit(solution)/shard_map/all_to_all | solution.py:51
  336.9 4.9 reshape_reshape_reshape.3
  341.9 4.6 fusion.10
  346.5 3.8 multiply_convert_fusion
  350.3 3.5 convolution_convert_fusion
  353.9 1.8 add_convert_fusion
  355.7 2.9 reshape_transpose_transpose_reshape_reshape_reshape_reshape.3
  358.5 107.1 %all_to_all.31 = bf16[128,1,1,6,2048]{4,3,2,1,0:T(8,128)(2,1)S(1)} all-to-all(bf16[128,1,1,6,2048]{4,3,2,1,0:T(8,128)(2,1)} %bitcast.114), channel_id=1, replica_groups=mesh['seq'=8,'expert'=16,'tensor'=2] {'seq','expert'}, dimensions={0} | all-to-all | bytes 6291456 | tf_op jit(solution)/shard_map/all_to_all | solution.py:51
  465.6 1.7 copy.75
  467.4 0.3 slice_bitcast_fusion.1
  467.7 1.9 pad_maximum_fusion.1
  469.6 4.3 all-to-all-start.5
  474.0 0.1 copy.77
  474.1 35.3 %all-to-all-done.5 = bf16[2,128,6,1024]{3,1,2,0:T(8,128)(2,1)S(1)} async-done(((bf16[2,128,6,1024]{3,1,2,0:T(8,128)(2,1)}), bf16[2,128,6,1024]{3,1,2,0:T(8,128)(2,1)S(1)}, u32[]{:S(2)}, u32[]{:S(2)}) %all-to-all-start.5) | async-done | bytes 3145760 | tf_op jit(solution)/shard_map/all_to_all | solution.py:175
  509.3 3.7 copy.76
  513.1 4.9 reshape_reshape.7
  518.0 5.4 %gather_fusion.1 = bf16[1024,1024]{1,0:T(8,128)(2,1)} fusion(bf16[1536,1024]{1,0:T(8,128)(2,1)S(1)} %reshape_reshape.7, s32[1024]{0:T(1024)S(1)} %broadcast_clamp_fusion), kind=kCustom, calls=%fused_computation.1 | custom fusion | bytes 4198400 | tf_op jit(solution)/shard_map/gather | solution.py:181
  523.3 2.9 fusion.4
  526.3 1.9 fusion.22
  (43 shorter events, 0.3 us)
Async XLA Ops:
  6.5 38.7 %all-gather.6.cloned.1.call-start = ((), (), s32[]{:S(2)}) async-start(), calls=%async_computation.6 | async-start | bytes 1179648 | tf_op jit(solution)/shard_map/all_gather | solution.py:14
  9.2 119.1 %all-gather.8.cloned.1.call-start = ((), (), s32[]{:S(2)}) async-start(), calls=%async_computation.7 | async-start | bytes 8912896 | tf_op jit(solution)/shard_map/all_gather | solution.py:115
  9.9 331.9 %all-gather.10.cloned.1.call-start = ((), (), s32[]{:S(2)}) async-start(), calls=%async_computation.8 | async-start | bytes 9437184 | tf_op jit(solution)/shard_map/all_gather | solution.py:14
  13.8 0.7 copy-start.4
  13.8 1.1 copy-start.2
  15.4 32.6 %copy-start.3 = (s32[128,9]{0,1:T(8,128)}, s32[128,9]{0,1:T(8,128)S(1)}, u32[]{:S(2)}) copy-start(s32[128,9]{0,1:T(8,128)S(1)} %reduce-window.9) | copy-start | bytes 13828
  128.3 9.0 %slice-start = ((s32[128,9]{0,1:T(8,128)}), s32[128,8]{0,1:T(8,128)S(1)}, s32[]{:S(2)}) async-start(s32[128,9]{0,1:T(8,128)} %copy-done.3), calls=%async_computation.10 | async-start | bytes 8192 | tf_op jit(solution)/shard_map/slice.1
  133.0 10.9 %copy-start.1 = (bf16[1,128,2048]{2,1,0:T(8,128)(2,1)S(1)}, bf16[1,128,2048]{2,1,0:T(8,128)(2,1)}, u32[]{:S(2)}) copy-start(bf16[1,128,2048]{2,1,0:T(8,128)(2,1)} %param.14) | copy-start | bytes 1572868
  133.0 19.3 %copy-start.5 = (f32[1024]{0:T(1024)S(1)}, f32[1024]{0:T(1024)}, u32[]{:S(2)}) copy-start(f32[1024]{0:T(1024)} %param.16) | copy-start | bytes 12292
  133.8 9.9 %all-to-all-start = ((bf16[2,128,1024]{2,1,0:T(8,128)(2,1)}), bf16[2,128,1024]{2,1,0:T(8,128)(2,1)S(1)}, u32[]{:S(2)}, u32[]{:S(2)}) async-start(bf16[2,128,1024]{2,1,0:T(8,128)(2,1)} %bitcast.112), calls=%async_computation | async-start | bytes 1048576 | tf_op jit(solution)/shard_map/all_to_all | solution.py:25
  143.9 26.3 %copy-start = (f32[128,1024]{1,0:T(8,128)}, f32[128,1024]{1,0:T(8,128)S(1)}, u32[]{:S(2)}) copy-start(f32[128,1024]{1,0:T(8,128)S(1)} %convert_reduce_fusion) | copy-start | bytes 1572868
  144.6 7.6 %all-to-all-start.1 = ((f32[2,1,128]{2,1,0:T(1,128)}), f32[2,1,128]{2,1,0:T(1,128)S(1)}, u32[]{:S(2)}, u32[]{:S(2)}) async-start(f32[2,1,128]{2,1,0:T(1,128)} %broadcast_in_dim.55), calls=%async_computation.1 | async-start | bytes 2048 | tf_op jit(solution)/shard_map/all_to_all | solution.py:31
  153.2 16.9 %all-to-all-start.2 = ((bf16[2,128,1024]{2,1,0:T(8,128)(2,1)}), bf16[2,128,1024]{2,1,0:T(8,128)(2,1)S(1)}, u32[]{:S(2)}, u32[]{:S(2)}) async-start(bf16[2,128,1024]{2,1,0:T(8,128)(2,1)} %broadcast_in_dim.56), calls=%async_computation.2 | async-start | bytes 1048576 | tf_op jit(solution)/shard_map/all_to_all | solution.py:31
  193.8 143.1 %all-to-all-start.3 = ((bf16[128,1,1,6,2048]{4,3,2,1,0:T(8,128)(2,1)}), bf16[128,1,1,6,2048]{4,3,2,1,0:T(8,128)(2,1)}, u32[]{:S(2)}, u32[]{:S(2)}) async-start(bf16[128,1,1,6,2048]{4,3,2,1,0:T(8,128)(2,1)} %fusion.3), calls=%async_computation.3 | async-start | bytes 8388608 | tf_op jit(solution)/shard_map/all_to_all | solution.py:51
  208.9 141.4 %all-gather.12.cloned.1.call-start = ((), (), s32[]{:S(2)}) async-start(), calls=%async_computation.9 | async-start | bytes 4718592 | tf_op jit(solution)/shard_map/all_gather | solution.py:84
  341.8 4.7 copy-start.7
  350.3 3.5 copy-start.8
  350.3 3.5 copy-start.9
  469.6 4.3 copy-start.6
  469.6 39.7 %all-to-all-start.5 = ((bf16[2,128,6,1024]{3,1,2,0:T(8,128)(2,1)}), bf16[2,128,6,1024]{3,1,2,0:T(8,128)(2,1)S(1)}, u32[]{:S(2)}, u32[]{:S(2)}) async-start(bf16[2,128,6,1024]{3,1,2,0:T(8,128)(2,1)} %pad_maximum_fusion.1), calls=%async_computation.5 | async-start | bytes 6291456 | tf_op jit(solution)/shard_map/all_to_all | solution.py:175
Sparse Core Ops, SparseCore 0:
  9.3 35.8 all-gather.5
  47.6 80.6 all-gather.7
  130.1 131.7 all-gather.9
  263.5 81.8 all-gather.11
